TPU v7x, 32 devices: a whole 2x2x4 slice. The times are simulated.
32 devices in a mesh: dp: 4 (over z), tensor: 8 (over y, x, core).
Axes of the slice: x: 2, y: 2, z: 4, core: 2. Of those that a mesh axis runs over, the one named last changes fastest.
Arguments:
- frames: bfloat16 [4, 16, 1024, 512], P(None, 'dp'), may hold values from -6 to 6
- cotangent: bfloat16 [4, 16, 1024, 512], P(None, 'dp'), may hold values from -6 to 6
- lengths: int32 [4, 16], P(None, 'dp'), may hold values from 1 to 1024, 12288 in all within a row
- expand_weight: float32 [512, 1536], P('dp', 'tensor'), may hold values from -0.25 to 0.25
- expand_first: float32 [512, 1536], P('dp', 'tensor'), may hold values from -384 to 384
- expand_second: float32 [512, 1536], P('dp', 'tensor'), may hold values from 3932.16 to 29491.2
- project_weight: float32 [1536, 512], P('tensor', 'dp'), may hold values from -0.15625 to 0.15625
- project_first: float32 [1536, 512], P('tensor', 'dp'), may hold values from -640 to 640
- project_second: float32 [1536, 512], P('tensor', 'dp'), may hold values from 9830.4 to 58982.4
- hidden_bias: float32 [1536], P('tensor'), may hold values from -3 to 3
- hidden_bias_first: float32 [1536], P('tensor'), may hold values from -384 to 384
- hidden_bias_second: float32 [1536], P('tensor'), may hold values from 3932.16 to 29491.2
- channel_param: float32 [12, 512], P(None, 'dp'), may hold values from -2 to 2
- channel_first: float32 [12, 512], P(None, 'dp'), may hold values from -768 to 768
- channel_second: float32 [12, 512], P(None, 'dp'), may hold values from 9830.4 to 73728
Outputs:
- block_out: bfloat16 [4, 16, 1024, 512], P(None, 'dp')
- frames_grad: bfloat16 [4, 16, 1024, 512], P(None, 'dp')
- expand_new: float32 [512, 1536], P('dp', 'tensor')
- expand_first_new: float32 [512, 1536], P('dp', 'tensor')
- expand_second_new: float32 [512, 1536], P('dp', 'tensor')
- expand_low: bfloat16 [512, 1536], P('dp', 'tensor')
- project_new: float32 [1536, 512], P('tensor', 'dp')
- project_first_new: float32 [1536, 512], P('tensor', 'dp')
- project_second_new: float32 [1536, 512], P('tensor', 'dp')
- project_low: bfloat16 [1536, 512], P('tensor', 'dp')
- bias_new: float32 [1536], P('tensor')
- bias_first_new: float32 [1536], P('tensor')
- bias_second_new: float32 [1536], P('tensor')
- channel_new: float32 [12, 512], P(None, 'dp')
- channel_first_new: float32 [12, 512], P(None, 'dp')
- channel_second_new: float32 [12, 512], P(None, 'dp')
Inputs may be any that keep to these rules, and one draw needn't show every extreme that they name: `lengths`: in each micro-batch the 16 true frame counts sum to 12288 and the largest is 1024.
All inputs are finite; a program needn't handle non-finite values. No bound on the sum of `lengths` on one device may be relied on, other than what follows from the above.
Results may differ from a plain program's by a relative error of at most 0.015.
Values may be sent and summed in bfloat16 or wider, within the bound.
A program may use at most 512 MiB of HBM per device.

v0:
```python
import jax
import jax.numpy as jnp
from jax import lax
from jax.sharding import PartitionSpec as P

eps_norm = 1e-06
beta_first = 0.5
beta_second = 0.5
adam_eps = 1e-08
decay_rate = 0.01
step_count = 6


def gelu_exact(value):
    return jax.nn.gelu(value, approximate=False)


def adam_update(weight, first, second, grad, rate):
    first_new = beta_first * first + (1.0 - beta_first) * grad
    second_new = beta_second * second + (1.0 - beta_second) * grad * grad
    first_hat = first_new / (1.0 - beta_first**step_count)
    second_hat = second_new / (1.0 - beta_second**step_count)
    weight_new = weight - rate * (
        first_hat / (jnp.sqrt(second_hat) + adam_eps) + decay_rate * weight
    )
    return (weight_new, first_new, second_new)


def contract_rows(left, right):
    return lax.dot_general(
        left, right, (((0,), (0,)), ((), ())), preferred_element_type=jnp.float32
    )


def contract_cols(left, right):
    return lax.dot_general(
        left, right, (((1,), (1,)), ((), ())), preferred_element_type=jnp.float32
    )


def per_device(
    frames,
    cotangent,
    lengths,
    expand_weight,
    expand_first,
    expand_second,
    project_weight,
    project_first,
    project_second,
    hidden_bias,
    hidden_bias_first,
    hidden_bias_second,
    channel_param,
    channel_first,
    channel_second,
):
    channel_full = lax.all_gather(channel_param, "dp", axis=1, tiled=True)
    taps = channel_full[0:7]
    kernel_bias = channel_full[7]
    norm_gain = channel_full[8]
    norm_shift = channel_full[9]
    out_bias = channel_full[10]
    layer_scale = channel_full[11]
    expand_bf = expand_weight.astype(jnp.bfloat16)
    project_bf = project_weight.astype(jnp.bfloat16)
    micro, clips, length, width = frames.shape
    hidden_part = expand_weight.shape[1]
    positions = lax.broadcasted_iota(jnp.int32, (clips, length), 1)
    grad_expand = jnp.zeros((width, hidden_part), jnp.float32)
    grad_project = jnp.zeros((hidden_part, width), jnp.float32)
    grad_channel = jnp.zeros((12, width), jnp.float32)
    grad_bias = jnp.zeros((hidden_part,), jnp.float32)
    out_list = []
    back_list = []
    for index in range(micro):
        expand_full, project_full = (
            lax.all_gather(expand_bf, "dp", axis=0, tiled=True),
            lax.all_gather(project_bf, "dp", axis=1, tiled=True),
        )
        mask = (positions < lengths[index][:, None]).astype(jnp.float32)[:, :, None]
        inputs = frames[index].astype(jnp.float32)
        masked = inputs * mask
        padded = jnp.pad(masked, ((0, 0), (3, 3), (0, 0)))
        conv = kernel_bias + sum((taps[k] * padded[:, k : k + length] for k in range(7)))
        mean = jnp.mean(conv, axis=-1, keepdims=True)
        centered = conv - mean
        var = jnp.mean(centered * centered, axis=-1, keepdims=True)
        inv_std = lax.rsqrt(var + eps_norm)
        nhat = centered * inv_std
        normed = (nhat * norm_gain + norm_shift).astype(jnp.bfloat16).reshape(clips * length, width)
        back = cotangent[index].astype(jnp.float32) * mask
        back_flat = back.reshape(clips * length, width)
        dz = layer_scale * back_flat
        dz_bf = dz.astype(jnp.bfloat16)
        pre = jnp.dot(normed, expand_full, preferred_element_type=jnp.float32) + hidden_bias
        gelu_out, gelu_back = jax.vjp(gelu_exact, pre)
        hidden = gelu_out.astype(jnp.bfloat16)
        partial_out = jnp.dot(hidden, project_full, preferred_element_type=jnp.float32)
        branch = lax.psum(partial_out.astype(jnp.bfloat16), "tensor").astype(jnp.float32)
        total = branch + out_bias
        piece_project = contract_rows(hidden, dz_bf)
        dhidden = contract_cols(dz_bf, project_full)
        dpre = gelu_back(dhidden)[0]
        piece_bias = jnp.sum(dpre, axis=0)
        dpre_bf = dpre.astype(jnp.bfloat16)
        piece_expand = contract_rows(normed, dpre_bf)
        dnormed_part = contract_cols(dpre_bf, expand_full)
        dnormed_flat = lax.psum(dnormed_part.astype(jnp.bfloat16), "tensor").astype(jnp.float32)
        outputs = (inputs + layer_scale * total.reshape(clips, length, width)) * mask
        out_list.append(outputs.astype(jnp.bfloat16))
        grad_scale = jnp.sum(back_flat * total, axis=0)
        grad_outb = jnp.sum(dz, axis=0)
        grad_bias = grad_bias + piece_bias
        dnormed = dnormed_flat.reshape(clips, length, width)
        grad_gain = jnp.sum(dnormed * nhat, axis=(0, 1))
        grad_shift = jnp.sum(dnormed, axis=(0, 1))
        dscaled = dnormed * norm_gain
        dconv = inv_std * (
            dscaled
            - jnp.mean(dscaled, axis=-1, keepdims=True)
            - nhat * jnp.mean(dscaled * nhat, axis=-1, keepdims=True)
        )
        grad_kbias = jnp.sum(dconv, axis=(0, 1))
        grad_taps = jnp.stack(
            [jnp.sum(dconv * padded[:, k : k + length], axis=(0, 1)) for k in range(7)], axis=0
        )
        dpadded = jnp.pad(dconv, ((0, 0), (3, 3), (0, 0)))
        dmasked = sum((taps[k] * dpadded[:, 6 - k : 6 - k + length] for k in range(7)))
        back_list.append((back + dmasked * mask).astype(jnp.bfloat16))
        piece_channel = jnp.concatenate(
            [
                grad_taps,
                grad_kbias[None],
                grad_gain[None],
                grad_shift[None],
                grad_outb[None],
                grad_scale[None],
            ],
            axis=0,
        )
        grad_expand = grad_expand + piece_expand
        grad_project = grad_project + piece_project
        grad_channel = grad_channel + piece_channel
    shard_expand, shard_project, shard_channel = (
        lax.psum_scatter(
            grad_expand.astype(jnp.bfloat16), "dp", scatter_dimension=0, tiled=True
        ).astype(jnp.float32),
        lax.psum_scatter(
            grad_project.astype(jnp.bfloat16), "dp", scatter_dimension=1, tiled=True
        ).astype(jnp.float32),
        lax.psum_scatter(
            grad_channel.astype(jnp.bfloat16), "dp", scatter_dimension=1, tiled=True
        ).astype(jnp.float32),
    )
    bias_total = lax.psum(grad_bias, "dp")
    e_new, e_first, e_second = adam_update(
        expand_weight, expand_first, expand_second, shard_expand, 0.02
    )
    p_new, p_first, p_second = adam_update(
        project_weight, project_first, project_second, shard_project, 0.01
    )
    b_new, b_first, b_second = adam_update(
        hidden_bias, hidden_bias_first, hidden_bias_second, bias_total, 0.1
    )
    c_new, c_first, c_second = adam_update(
        channel_param, channel_first, channel_second, shard_channel, 0.2
    )
    return (
        jnp.stack(out_list, axis=0),
        jnp.stack(back_list, axis=0),
        e_new,
        e_first,
        e_second,
        e_new.astype(jnp.bfloat16),
        p_new,
        p_first,
        p_second,
        p_new.astype(jnp.bfloat16),
        b_new,
        b_first,
        b_second,
        c_new,
        c_first,
        c_second,
    )


def solution(mesh):
    in_specs = (
        P(None, "dp", None, None),
        P(None, "dp", None, None),
        P(None, "dp"),
        P("dp", "tensor"),
        P("dp", "tensor"),
        P("dp", "tensor"),
        P("tensor", "dp"),
        P("tensor", "dp"),
        P("tensor", "dp"),
        P("tensor"),
        P("tensor"),
        P("tensor"),
        P(None, "dp"),
        P(None, "dp"),
        P(None, "dp"),
    )
    out_specs = (
        P(None, "dp", None, None),
        P(None, "dp", None, None),
        P("dp", "tensor"),
        P("dp", "tensor"),
        P("dp", "tensor"),
        P("dp", "tensor"),
        P("tensor", "dp"),
        P("tensor", "dp"),
        P("tensor", "dp"),
        P("tensor", "dp"),
        P("tensor"),
        P("tensor"),
        P("tensor"),
        P(None, "dp"),
        P(None, "dp"),
        P(None, "dp"),
    )
    return jax.shard_map(
        per_device, mesh=mesh, in_specs=in_specs, out_specs=out_specs, check_vma=False
    )
```

profile of v0, /device:TPU:0, one launch (start us, length us, event | category | flops | bytes accessed | tf_op | source)
XLA Modules:
  0.0 1032.3 jit_solution(2472263985125396175)
XLA Ops:
  8.9 15.0 %all_gather.6 = f32[12,512]{1,0:T(8,128)S(1)} all-gather(f32[12,128]{1,0:T(8,128)} %param.27), channel_id=1, replica_groups=mesh['dp'=4,'tensor'=8] {'dp'}, dimensions={1}, use_global_device_ids=true | all-gather | bytes 30720 | tf_op jit(solution)/shard_map/all_gather | solution.py:58
  28.4 13.4 %all_gather.8 = bf16[192,512]{1,0:T(8,128)(2,1)} all-gather(bf16[192,128]{1,0:T(8,128)(2,1)S(1)} %convert_element_type.318), channel_id=1, replica_groups=mesh['dp'=4,'tensor'=8] {'dp'}, dimensions={1}, use_global_device_ids=true | all-gather | bytes 245760 | tf_op jit(solution)/shard_map/all_gather | solution.py:79
  41.7 13.1 %all_gather.7 = bf16[512,192]{0,1:T(8,128)(2,1)} all-gather(bf16[128,192]{0,1:T(8,128)(2,1)S(1)} %convert_element_type.316), channel_id=1, replica_groups=mesh['dp'=4,'tensor'=8] {'dp'}, dimensions={0}, use_global_device_ids=true | all-gather | bytes 245760 | tf_op jit(solution)/shard_map/all_gather | solution.py:78
  54.9 16.1 %fusion.2 = (f32[4,1024,512]{2,1,0:T(8,128)}, f32[4,1024,512]{2,1,0:T(8,128)}, f32[4,1024,512]{2,1,0:T(8,128)}, f32[4,1024,512]{2,1,0:T(8,128)}) fusion(f32[4,1024]{1,0:T(4,128)S(1)} %get-tuple-element.190, bf16[4,4,1024,512]{3,2,1,0:T(8,128)(2,1)} %param.15, f32[4,1024]{1,0:T(4,128)S(1)} %get-tuple-element.199, f32[4,1024]{1,0:T(4,128)S(1)} %get-tuple-element.194, ...), kind=kLoop, calls=%fused_computation.12 | loop fusion | flops 16777216 | bytes 50397184 | tf_op jit(solution)/shard_map/mul | solution.py:83
  71.1 82.5 %fusion.97 = (f32[4,1024]{1,0:T(4,128)S(1)}, f32[4,1024,512]{2,1,0:T(8,128)S(1)}, f32[4,1024]{1,0:T(4,128)S(1)}, f32[4,1024,512]{2,1,0:T(8,128)S(1)}, f32[4,1024...) fusion(f32[512]{0:T(512)S(1)} %bitcast.296, f32[512]{0:T(512)S(1)} %bitcast.299, ...), kind=kLoop, calls=%fused_computation.319 | loop fusion | flops 125812736 | bytes 67190784 | tf_op jit(solution)/shard_map/reduce_sum | solution.py:86
  153.7 9.9 multiply_reduce_fusion.48
  170.6 7.9 add_convert_fusion.3
  178.6 6.9 convolution_add_fusion.2
  188.7 3.3 convolution_add_fusion.1
  195.3 7.2 multiply_convert_fusion.3
  202.5 10.7 %fusion.91 = (f32[192]{0:T(256)}, bf16[4096,192]{0,1:T(8,128)(2,1)}, f32[4096,192]{0,1:T(8,128)S(1)}) fusion(f32[4096,192]{0,1:T(8,128)S(1)} %copy-done.29, bf16[4096,512]{1,0:T(8,128)(2,1)S(1)} %get-tuple-element.134, bf16[192,512]{1,0:T(8,128)(2,1)S(1)} %copy-done.38), kind=kOutput, calls=%fused_computation.316 | convolution fusion | flops 862715712 | bytes 12256000 | tf_op jit(solution)/shard_map/dot_general | solution.py:36
  215.1 9.6 fusion.89
  227.9 9.6 fusion.87
  240.4 9.8 fusion.85
  254.6 3.8 fusion.68
  264.9 3.3 convolution_convert_fusion.4
  274.7 3.3 convolution_convert_fusion.1
  281.3 3.3 convolution_convert_fusion.3
  291.8 9.4 psum.71
  305.3 388.8 %all-reduce.11.cloned.1.call-done = (bf16[4096,512]{1,0:T(8,128)(2,1)}, bf16[4096,512]{1,0:T(8,128)(2,1)}, bf16[4096,512]{1,0:T(8,128)(2,1)}, bf16[4096,512]{1,0...) async-done(((bf16[4096,512]{1,0:T(8,128)(2,1)}, bf16[4096,512]{1,0:T(8,128)(2,1)}, ...) | async-done | bytes 33554448 | tf_op jit(solution)/shard_map/psum | solution.py:100
  694.1 15.6 %multiply_reduce_fusion.12 = (f32[512]{0:T(512)S(1)}, f32[4,1024]{1,0:T(4,128)S(1)}, f32[4,1024]{1,0:T(4,128)S(1)}, f32[512]{0:T(512)S(1)}) fusion(f32[4,1024,512]{2,1,0:T(8,128)} %get-tuple-element.162, f32[4,1024]{1,0:T(4,128)S(1)} %copy-done.62, f32[4,1024]{1,0:T(4,128)S(1)} %copy-done.44, bf16[4096,512]{1,0:T(8,128)(2,1)} %get-tuple-element.83, ...), kind=kLoop, calls=%fused_computation.50 | loop fusion | flops 37739520 | bytes 33658880 | tf_op jit(solution)/shard_map/reduce_sum | solution.py:116
  709.8 4.8 convert_reduce_fusion
  714.8 40.5 %multiply_reduce_fusion.13 = (f32[512]{0:T(512)S(1)}, f32[512]{0:T(512)S(1)}, f32[512]{0:T(512)S(1)}, f32[512]{0:T(512)S(1)}, f32[512]{0:T(512)S(1)}, /*index=5*...) fusion(f32[4,1024,512]{2,1,0:T(8,128)} %get-tuple-element.137, ...), kind=kLoop, calls=%fused_computation.51 | loop fusion | flops 60809728 | bytes 46268416 | tf_op jit(solution)/shard_map/reduce_sum | solution.py:126
  755.4 42.4 %multiply_reduce_fusion.2 = (f32[512]{0:T(512)S(1)}, f32[4,1024]{1,0:T(4,128)S(1)}, f32[512]{0:T(512)S(1)}, f32[512]{0:T(512)S(1)}, f32[512]{0:T(512)S(1)}, /*in...) fusion(f32[4,1024,512]{2,1,0:T(8,128)} %get-tuple-element.164, ...), kind=kLoop, calls=%fused_computation.40 | loop fusion | flops 60809728 | bytes 46268416 | tf_op jit(solution)/shard_map/reduce_sum | solution.py:116
  797.9 28.1 %multiply_reduce_fusion.23 = (f32[512]{0:T(512)S(1)}, f32[512]{0:T(512)S(1)}, f32[512]{0:T(512)S(1)}, f32[512]{0:T(512)S(1)}, f32[512]{0:T(512)S(1)}, /*index=5*...) fusion(f32[4,1024,512]{2,1,0:T(8,128)} %get-tuple-element.136, f32[4,1024]{1,0:T(4,128)S(1)} %broadcast_multiply_fusion.6, ...), kind=kLoop, calls=%fused_computation.61 | loop fusion | flops 44036608 | bytes 29442048 | tf_op jit(solution)/shard_map/reduce_sum | solution.py:126
  826.1 67.0 %fusion.32 = (bf16[1,4,1024,512]{3,2,1,0:T(8,128)(2,1)}, bf16[1,4,1024,512]{3,2,1,0:T(8,128)(2,1)}, bf16[1,4,1024,512]{3,2,1,0:T(8,128)(2,1)}) fusion(f32[4,1024]{1,0:T(4,128)S(1)} %copy-done.48, f32[512]{0:T(512)S(1)} %bitcast.297, f32[512]{0:T(512)S(1)} %bitcast.300, f32[512]{0:T(512)S(1)} %bitcast.303, f32[4,1024,512]{2,1,0:T(8,128)} %get-tuple-element.181, ...), kind=kLoop, calls=%fused_computation.174 | loop fusion | flops 106954752 | bytes 50395136 | tf_op jit(solution)/shard_map/stack | solution.py:171
  893.1 48.9 %multiply_reduce_fusion.26 = (f32[512]{0:T(512)S(1)}, f32[512]{0:T(512)S(1)}, f32[512]{0:T(512)S(1)}, f32[512]{0:T(512)S(1)}, f32[512]{0:T(512)S(1)}, /*index=5*...) fusion(f32[4,1024,512]{2,1,0:T(8,128)} %get-tuple-element.89, ...), kind=kLoop, calls=%fused_computation.64 | loop fusion | flops 81782272 | bytes 71462912 | tf_op jit(solution)/shard_map/reduce_sum | solution.py:126
  942.1 10.2 fusion.35
  952.3 19.5 %multiply_reduce_fusion.20 = (f32[512]{0:T(512)S(1)}, f32[512]{0:T(512)S(1)}, f32[512]{0:T(512)S(1)}, f32[512]{0:T(512)S(1)}, f32[4096,512]{1,0:T(8,128)S(1)}, /...) fusion(f32[4096]{0:T(1024)S(1)} %bitcast.282, bf16[4,4,1024,512]{3,2,1,0:T(8,128)(2,1)} %param.16, ...), kind=kLoop, calls=%fused_computation.58 | loop fusion | flops 50329600 | bytes 67184640 | tf_op jit(solution)/shard_map/reduce_sum | solution.py:112
  971.7 26.7 %fusion.1 = (bf16[1,4,1024,512]{3,2,1,0:T(8,128)(2,1)}, bf16[1,4,1024,512]{3,2,1,0:T(8,128)(2,1)}, bf16[1,4,1024,512]{3,2,1,0:T(8,128)(2,1)}, bf16[1,4,1024,512]...) fusion(f32[4,1024]{1,0:T(4,128)S(1)} %copy-done.48, ...), kind=kLoop, calls=%fused_computation.11 | loop fusion | flops 75495424 | bytes 83961856 | tf_op jit(solution)/shard_map/convert_element_type | solution.py:111
  999.5 16.8 %pad_maximum_fusion.1 = bf16[4,4,1024,512]{3,2,1,0:T(8,128)(2,1)} fusion(bf16[1,4,1024,512]{3,2,1,0:T(8,128)(2,1)} %fusion.35, bf16[1,4,1024,512]{3,2,1,0:T(8,128)(2,1)} %get-tuple-element.126, bf16[1,4,1024,512]{3,2,1,0:T(8,128)(2,1)} %get-tuple-element.125, bf16[1,4,1024,512]{3,2,1,0:T(8,128)(2,1)} %get-tuple-element.124), kind=kLoop, calls=%fused_computation.1 | loop fusion | flops 25165824 | bytes 33554432 | tf_op jit(solution)/shard_map/stack | solution.py:171
  1016.4 7.0 pad_maximum_fusion
  (294 shorter events, 60.8 us)
Async XLA Ops:
  8.0 293.8 %reduce-scatter.12.cloned.1.call-start = ((), (), s32[]{:S(2)}) async-start(), calls=%async_computation.4 | async-start | bytes 327680
  24.5 46.6 %copy-start.79 = (f32[1,512]{1,0:T(1,128)}, f32[1,512]{1,0:T(1,128)S(1)}, u32[]{:S(2)}) copy-start(f32[1,512]{1,0:T(1,128)S(1)} %get-tuple-element.150) | copy-start | bytes 6148
  24.5 46.6 %copy-start.81 = (f32[1,512]{1,0:T(1,128)}, f32[1,512]{1,0:T(1,128)S(1)}, u32[]{:S(2)}) copy-start(f32[1,512]{1,0:T(1,128)S(1)} %get-tuple-element.151) | copy-start | bytes 6148
  24.5 46.6 %copy-start.83 = (f32[1,512]{1,0:T(1,128)}, f32[1,512]{1,0:T(1,128)S(1)}, u32[]{:S(2)}) copy-start(f32[1,512]{1,0:T(1,128)S(1)} %get-tuple-element.152) | copy-start | bytes 6148
  24.5 46.6 %copy-start.85 = (f32[1,512]{1,0:T(1,128)}, f32[1,512]{1,0:T(1,128)S(1)}, u32[]{:S(2)}) copy-start(f32[1,512]{1,0:T(1,128)S(1)} %get-tuple-element.153) | copy-start | bytes 6148
  24.5 46.6 %copy-start.87 = (f32[1,512]{1,0:T(1,128)}, f32[1,512]{1,0:T(1,128)S(1)}, u32[]{:S(2)}) copy-start(f32[1,512]{1,0:T(1,128)S(1)} %get-tuple-element.154) | copy-start | bytes 6148
  24.5 46.6 %copy-start.89 = (f32[1,512]{1,0:T(1,128)}, f32[1,512]{1,0:T(1,128)S(1)}, u32[]{:S(2)}) copy-start(f32[1,512]{1,0:T(1,128)S(1)} %get-tuple-element.155) | copy-start | bytes 6148
  24.5 46.6 %copy-start.91 = (f32[1,512]{1,0:T(1,128)}, f32[1,512]{1,0:T(1,128)S(1)}, u32[]{:S(2)}) copy-start(f32[1,512]{1,0:T(1,128)S(1)} %get-tuple-element.156) | copy-start | bytes 6148
  24.5 145.2 %copy-start.70 = (f32[1,512]{1,0:T(1,128)}, f32[1,512]{1,0:T(1,128)S(1)}, u32[]{:S(2)}) copy-start(f32[1,512]{1,0:T(1,128)S(1)} %get-tuple-element.149) | copy-start | bytes 6148
  26.4 44.6 %copy-start.47 = (f32[4,1024]{1,0:T(4,128)}, f32[4,1024]{1,0:T(4,128)S(1)}, u32[]{:S(2)}) copy-start(f32[4,1024]{1,0:T(4,128)S(1)} %get-tuple-element.190) | copy-start | bytes 49156
  26.4 44.6 %copy-start.49 = (f32[4,1024]{1,0:T(4,128)}, f32[4,1024]{1,0:T(4,128)S(1)}, u32[]{:S(2)}) copy-start(f32[4,1024]{1,0:T(4,128)S(1)} %get-tuple-element.199) | copy-start | bytes 49156
  26.5 168.8 %copy-start.65 = (f32[1,8,4,128]{3,1,2,0:T(8,128)}, f32[1,8,4,128]{3,1,2,0:T(8,128)S(1)}, u32[]{:S(2)}) copy-start(f32[1,8,4,128]{3,1,2,0:T(8,128)S(1)} %copy.48) | copy-start | bytes 49156
  27.1 43.9 %copy-start.51 = (f32[4,1024]{1,0:T(4,128)}, f32[4,1024]{1,0:T(4,128)S(1)}, u32[]{:S(2)}) copy-start(f32[4,1024]{1,0:T(4,128)S(1)} %get-tuple-element.194) | copy-start | bytes 49156
  27.2 43.9 %copy-start.53 = (f32[4,1024]{1,0:T(4,128)}, f32[4,1024]{1,0:T(4,128)S(1)}, u32[]{:S(2)}) copy-start(f32[4,1024]{1,0:T(4,128)S(1)} %get-tuple-element.201) | copy-start | bytes 49156
  254.6 48.2 %reduce-scatter.10.cloned.1.call-start = ((), (), s32[]{:S(2)}) async-start(), calls=%async_computation.3 | async-start | bytes 327680
  264.8 429.3 %all-reduce.11.cloned.1.call-start = ((), (), s32[]{:S(2)}) async-start(), calls=%async_computation.6 | async-start | bytes 67108864 | tf_op jit(solution)/shard_map/psum | solution.py:100
  291.2 402.9 %copy-start.42 = (f32[4,1024]{1,0:T(4,128)S(1)}, f32[4,1024]{1,0:T(4,128)}, u32[]{:S(2)}) copy-start(f32[4,1024]{1,0:T(4,128)} %copy-done.41) | copy-start | bytes 49156
  291.2 402.9 %copy-start.44 = (f32[4,1024]{1,0:T(4,128)S(1)}, f32[4,1024]{1,0:T(4,128)}, u32[]{:S(2)}) copy-start(f32[4,1024]{1,0:T(4,128)} %copy-done.43) | copy-start | bytes 49156
  291.2 402.9 %copy-start.60 = (f32[4,1024]{1,0:T(4,128)S(1)}, f32[4,1024]{1,0:T(4,128)}, u32[]{:S(2)}) copy-start(f32[4,1024]{1,0:T(4,128)} %copy-done.59) | copy-start | bytes 49156
  291.2 402.9 %copy-start.62 = (f32[4,1024]{1,0:T(4,128)S(1)}, f32[4,1024]{1,0:T(4,128)}, u32[]{:S(2)}) copy-start(f32[4,1024]{1,0:T(4,128)} %copy-done.61) | copy-start | bytes 49156
  291.2 402.9 %copy-start.71 = (f32[1,512]{1,0:T(1,128)S(1)}, f32[1,512]{1,0:T(1,128)}, u32[]{:S(2)}) copy-start(f32[1,512]{1,0:T(1,128)} %copy-done.70) | copy-start | bytes 6148
  291.2 732.2 %reduce-scatter.14.cloned.1.call-start = ((), (), s32[]{:S(2)}) async-start(), calls=%async_computation.5 | async-start | bytes 163840
  714.7 40.6 %copy-start.46 = (f32[4,1024]{1,0:T(4,128)S(1)}, f32[4,1024]{1,0:T(4,128)}, u32[]{:S(2)}) copy-start(f32[4,1024]{1,0:T(4,128)} %copy-done.45) | copy-start | bytes 49156
  714.7 40.6 %copy-start.64 = (f32[4,1024]{1,0:T(4,128)S(1)}, f32[4,1024]{1,0:T(4,128)}, u32[]{:S(2)}) copy-start(f32[4,1024]{1,0:T(4,128)} %copy-done.63) | copy-start | bytes 49156
  755.4 42.4 %copy-start.4 = (bf16[4096,512]{1,0:T(8,128)(2,1)S(1)}, bf16[4096,512]{1,0:T(8,128)(2,1)}, u32[]{:S(2)}) copy-start(bf16[4096,512]{1,0:T(8,128)(2,1)} %get-tuple-element.84) | copy-start | bytes 12582916
  797.8 28.2 %copy-start.48 = (f32[4,1024]{1,0:T(4,128)S(1)}, f32[4,1024]{1,0:T(4,128)}, u32[]{:S(2)}) copy-start(f32[4,1024]{1,0:T(4,128)} %copy-done.47) | copy-start | bytes 49156
  797.8 28.2 %copy-start.50 = (f32[4,1024]{1,0:T(4,128)S(1)}, f32[4,1024]{1,0:T(4,128)}, u32[]{:S(2)}) copy-start(f32[4,1024]{1,0:T(4,128)} %copy-done.49) | copy-start | bytes 49156
  797.8 28.2 %copy-start.52 = (f32[4,1024]{1,0:T(4,128)S(1)}, f32[4,1024]{1,0:T(4,128)}, u32[]{:S(2)}) copy-start(f32[4,1024]{1,0:T(4,128)} %copy-done.51) | copy-start | bytes 49156
  797.8 28.2 %copy-start.80 = (f32[1,512]{1,0:T(1,128)S(1)}, f32[1,512]{1,0:T(1,128)}, u32[]{:S(2)}) copy-start(f32[1,512]{1,0:T(1,128)} %copy-done.79) | copy-start | bytes 6148
  797.8 28.2 %copy-start.82 = (f32[1,512]{1,0:T(1,128)S(1)}, f32[1,512]{1,0:T(1,128)}, u32[]{:S(2)}) copy-start(f32[1,512]{1,0:T(1,128)} %copy-done.81) | copy-start | bytes 6148
  797.9 28.2 %copy-start.84 = (f32[1,512]{1,0:T(1,128)S(1)}, f32[1,512]{1,0:T(1,128)}, u32[]{:S(2)}) copy-start(f32[1,512]{1,0:T(1,128)} %copy-done.83) | copy-start | bytes 6148
  826.1 67.0 %copy-start.54 = (f32[4,1024]{1,0:T(4,128)S(1)}, f32[4,1024]{1,0:T(4,128)}, u32[]{:S(2)}) copy-start(f32[4,1024]{1,0:T(4,128)} %copy-done.53) | copy-start | bytes 49156
  (79 other events, 761.9 us)
Sparse Core Ops, SparseCore 0:
  254.7 18.2 reduce-scatter.11
  275.2 17.8 reduce-scatter.9
  999.6 19.1 reduce-scatter.13
Sparse Core Ops, SparseCore 1:
  291.3 402.7 all-reduce.10
where the time goes:
time: 1040 us; the launch traced here: 1030 us
  other arithmetic  462 us (44%)
  waiting for transfers between devices  389 us (37%)
  matrix products  93.3 us (9%)
  blocking collectives  50.9 us (5%)
  local copies, waits for them, and re-layouts  20.1 us (2%)
  between operations  17 us (2%)
    psum x1, waiting for transfers between devices, per_device(): lax.psum(partial_out.astype(jnp.bfloat16), 'tensor').astype(jnp.float32)  389 us
    reduce_sum x3, other arithmetic, per_device(): jnp.sum(dconv * padded[:, k:k + length], axis=(0, 1))  118 us
    another operation x3, other arithmetic, per_device(): jnp.stack(back_list, axis=0)  94 us
    reduce_sum x1, other arithmetic, per_device(): mean = jnp.mean(conv, axis=-1, keepdims=True)  82.5 us
    reduce_sum x2, other arithmetic, per_device(): grad_gain = jnp.sum(dnormed * nhat, axis=(0, 1))  58 us
    dot_general x8, matrix products, contract_cols(): lax.dot_general(left, right, (((1,), (1,)), ((), ())), preferred_element_...  52.8 us
    convert_element_type x1, other arithmetic, per_device(): out_list.append(outputs.astype(jnp.bfloat16))  26.7 us
  transfers between devices with their start and end apart: 4, of which 1 were waited for; matrix products, arithmetic and copies ran while one was open for 6% of the time, Pallas kernels for 0%

commit v1 on v0

--- a/solution.py
+++ b/solution.py
@@ -97,7 +97,9 @@
         gelu_out, gelu_back = jax.vjp(gelu_exact, pre)
         hidden = gelu_out.astype(jnp.bfloat16)
         partial_out = jnp.dot(hidden, project_full, preferred_element_type=jnp.float32)
-        branch = lax.psum(partial_out.astype(jnp.bfloat16), "tensor").astype(jnp.float32)
+        branch = jnp.sum(lax.all_gather(partial_out.astype(jnp.bfloat16), "tensor"), axis=0).astype(
+            jnp.float32
+        )
         total = branch + out_bias
         piece_project = contract_rows(hidden, dz_bf)
         dhidden = contract_cols(dz_bf, project_full)

time: 1040 us -> 1220 us (1.17)
  waiting for transfers between devices: 389 us -> 498 us
  other arithmetic: 462 us -> 518 us
    all_gather x0 -> x4, waiting for transfers between devices: none -> 310 us  [per_device(): lax.all_gather(partial_out.astype(jnp.bfloat16), 'tensor')]
    psum x1, waiting for transfers between devices: 389 us -> 188 us  [per_device(): lax.psum(dnormed_part.astype(jnp.bfloat16), 'tensor').astype(jnp.float32)]
    reduce_sum x0 -> x4, other arithmetic: none -> 62 us  [per_device(): jnp.sum(lax.all_gather(partial_out.astype(jnp.bfloat16), 'tensor'), axis=0)]
    another operation x3, other arithmetic: 94 us -> 111 us  [per_device(): jnp.stack(back_list, axis=0)]
    convert_element_type x1, other arithmetic: 26.7 us -> 13.5 us  [per_device(): out_list.append(outputs.astype(jnp.bfloat16))]
  transfers between devices with their start and end apart: 4 -> 8, of which waited for: 1 -> 4; matrix products, arithmetic and copies ran while one was open for 6% -> 34% of each run, Pallas kernels for 0% -> 0%
where the time goes in v1:
time: 1220 us; the launch traced here: 1210 us
  other arithmetic  518 us (42%)
  waiting for transfers between devices  498 us (41%)
  matrix products  101 us (8%)
  blocking collectives  50.1 us (4%)
  local copies, waits for them, and re-layouts  22.1 us (2%)
  between operations  17.3 us (1%)
    all_gather x4, waiting for transfers between devices, per_device(): lax.all_gather(partial_out.astype(jnp.bfloat16), 'tensor')  310 us
    psum x1, waiting for transfers between devices, per_device(): lax.psum(dnormed_part.astype(jnp.bfloat16), 'tensor').astype(jnp.float32)  188 us
    reduce_sum x3, other arithmetic, per_device(): jnp.sum(dconv * padded[:, k:k + length], axis=(0, 1))  114 us
    another operation x3, other arithmetic, per_device(): jnp.stack(back_list, axis=0)  111 us
    reduce_sum x1, other arithmetic, per_device(): mean = jnp.mean(conv, axis=-1, keepdims=True)  80.7 us
    reduce_sum x4, other arithmetic, per_device(): jnp.sum(lax.all_gather(partial_out.astype(jnp.bfloat16), 'tensor'), axis=0)  62 us
    reduce_sum x2, other arithmetic, per_device(): grad_gain = jnp.sum(dnormed * nhat, axis=(0, 1))  58.4 us
    dot_general x8, matrix products, contract_cols(): lax.dot_general(left, right, (((1,), (1,)), ((), ())), preferred_element_...  57.1 us
  transfers between devices with their start and end apart: 8, of which 4 were waited for; matrix products, arithmetic and copies ran while one was open for 34% of the time, Pallas kernels for 0%

profile of v1, /device:TPU:0, one launch (start us, length us, event | category | flops | bytes accessed | tf_op | source)
XLA Modules:
  0.0 1207.6 jit_solution(2143564541400887137)
XLA Ops:
  8.9 15.0 %all_gather.39 = f32[12,512]{1,0:T(8,128)S(1)} all-gather(f32[12,128]{1,0:T(8,128)} %param.27), channel_id=1, replica_groups=mesh['dp'=4,'tensor'=8] {'dp'}, dimensions={1}, use_global_device_ids=true | all-gather | bytes 30720 | tf_op jit(solution)/shard_map/all_gather | solution.py:58
  28.4 13.4 %all_gather.41 = bf16[192,512]{1,0:T(8,128)(2,1)} all-gather(bf16[192,128]{1,0:T(8,128)(2,1)S(1)} %convert_element_type.390), channel_id=1, replica_groups=mesh['dp'=4,'tensor'=8] {'dp'}, dimensions={1}, use_global_device_ids=true | all-gather | bytes 245760 | tf_op jit(solution)/shard_map/all_gather | solution.py:79
  41.7 13.1 %all_gather.40 = bf16[512,192]{0,1:T(8,128)(2,1)} all-gather(bf16[128,192]{0,1:T(8,128)(2,1)S(1)} %convert_element_type.388), channel_id=1, replica_groups=mesh['dp'=4,'tensor'=8] {'dp'}, dimensions={0}, use_global_device_ids=true | all-gather | bytes 245760 | tf_op jit(solution)/shard_map/all_gather | solution.py:78
  54.9 16.1 %fusion.2 = (f32[4,1024,512]{2,1,0:T(8,128)}, f32[4,1024,512]{2,1,0:T(8,128)}, f32[4,1024,512]{2,1,0:T(8,128)}, f32[4,1024,512]{2,1,0:T(8,128)}) fusion(f32[4,1024]{1,0:T(4,128)S(1)} %get-tuple-element.184, bf16[4,4,1024,512]{3,2,1,0:T(8,128)(2,1)} %param.15, f32[4,1024]{1,0:T(4,128)S(1)} %get-tuple-element.193, f32[4,1024]{1,0:T(4,128)S(1)} %get-tuple-element.188, ...), kind=kLoop, calls=%fused_computation.12 | loop fusion | flops 16777216 | bytes 50397184 | tf_op jit(solution)/shard_map/mul | solution.py:83
  71.1 80.7 %fusion.117 = (f32[4,1024]{1,0:T(4,128)S(1)}, f32[4,1024,512]{2,1,0:T(8,128)S(1)}, f32[4,1024]{1,0:T(4,128)S(1)}, f32[4,1024,512]{2,1,0:T(8,128)S(1)}, f32[4,102...) fusion(f32[512]{0:T(512)S(1)} %bitcast.313, f32[512]{0:T(512)S(1)} %bitcast.316, ...), kind=kLoop, calls=%fused_computation.331 | loop fusion | flops 125812736 | bytes 67190784 | tf_op jit(solution)/shard_map/reduce_sum | solution.py:86
  152.0 9.9 multiply_reduce_fusion.44
  168.8 8.0 add_convert_fusion.3
  199.7 13.1 %fusion.111 = (f32[192]{0:T(256)}, bf16[4096,192]{0,1:T(8,128)(2,1)}, f32[4096,192]{0,1:T(8,128)S(1)}) fusion(f32[4096,192]{0,1:T(8,128)} %convolution_add_fusion, bf16[4096,512]{1,0:T(8,128)(2,1)S(1)} %get-tuple-element.136, bf16[192,512]{1,0:T(8,128)(2,1)S(1)} %copy-done.28), kind=kOutput, calls=%fused_computation.328 | convolution fusion | flops 862715712 | bytes 12256000 | tf_op jit(solution)/shard_map/dot_general | solution.py:36
  215.2 9.6 fusion.109
  227.3 9.7 fusion.107
  241.1 10.0 fusion.105
  299.5 8.6 psum.39
  312.2 187.7 %all-reduce.11.cloned.1.call-done = (bf16[4096,512]{1,0:T(8,128)(2,1)}, bf16[4096,512]{1,0:T(8,128)(2,1)}, bf16[4096,512]{1,0:T(8,128)(2,1)}, bf16[4096,512]{1,0:T(8,128)(2,1)}) async-done(((bf16[4096,512]{1,0:T(8,128)(2,1)}, bf16[4096,512]{1,0:T(8,128)(2,1)}, bf16[4096,512]{1,0:T(8,128)(2,1)}, bf16[4096,512]{1,0:T(8,128)(2,1)}), (bf16[4096,512]{1,0:T(8,128)(2,1)}, bf16[4096,512]{1,0:T(8,128)(2,1)}, ...) | async-done | bytes 16777232 | tf_op jit(solution)/shard_map/psum | solution.py:111
  499.9 8.3 convert_reduce_fusion
  508.4 16.5 %multiply_reduce_fusion.10 = (f32[512]{0:T(512)S(1)}, f32[4,1024]{1,0:T(4,128)S(1)}, f32[4,1024]{1,0:T(4,128)S(1)}, f32[512]{0:T(512)S(1)}) fusion(f32[4,1024,512]{2,1,0:T(8,128)} %get-tuple-element.156, f32[4,1024]{1,0:T(4,128)S(1)} %copy-done.52, f32[4,1024]{1,0:T(4,128)S(1)} %copy-done.42, bf16[4096,512]{1,0:T(8,128)(2,1)} %get-tuple-element.85, ...), kind=kLoop, calls=%fused_computation.72 | loop fusion | flops 37739520 | bytes 33658880 | tf_op jit(solution)/shard_map/reduce_sum | solution.py:118
  525.0 34.9 %multiply_reduce_fusion.11 = (f32[512]{0:T(512)S(1)}, f32[512]{0:T(512)S(1)}, f32[512]{0:T(512)S(1)}, f32[512]{0:T(512)S(1)}, f32[512]{0:T(512)S(1)}, /*index=5*...) fusion(f32[4,1024,512]{2,1,0:T(8,128)} %get-tuple-element.139, ...), kind=kLoop, calls=%fused_computation.73 | loop fusion | flops 60809728 | bytes 46268416 | tf_op jit(solution)/shard_map/reduce_sum | solution.py:128
  559.9 41.9 %multiply_reduce_fusion.1 = (f32[512]{0:T(512)S(1)}, f32[4,1024]{1,0:T(4,128)S(1)}, f32[512]{0:T(512)S(1)}, f32[512]{0:T(512)S(1)}, f32[512]{0:T(512)S(1)}, /*in...) fusion(f32[4,1024,512]{2,1,0:T(8,128)} %get-tuple-element.158, ...), kind=kLoop, calls=%fused_computation.63 | loop fusion | flops 60809728 | bytes 46268416 | tf_op jit(solution)/shard_map/reduce_sum | solution.py:118
  601.9 32.8 %multiply_reduce_fusion.20 = (f32[512]{0:T(512)S(1)}, f32[512]{0:T(512)S(1)}, f32[512]{0:T(512)S(1)}, f32[512]{0:T(512)S(1)}, f32[512]{0:T(512)S(1)}, /*index=5*...) fusion(f32[4,1024,512]{2,1,0:T(8,128)} %get-tuple-element.138, f32[4,1024]{1,0:T(4,128)S(1)} %broadcast_multiply_fusion.6, ...), kind=kLoop, calls=%fused_computation.82 | loop fusion | flops 44036608 | bytes 29442048 | tf_op jit(solution)/shard_map/reduce_sum | solution.py:128
  634.9 46.8 %multiply_reduce_fusion.23 = (f32[512]{0:T(512)S(1)}, f32[512]{0:T(512)S(1)}, f32[512]{0:T(512)S(1)}, f32[512]{0:T(512)S(1)}, f32[512]{0:T(512)S(1)}, /*index=5*...) fusion(f32[4,1024,512]{2,1,0:T(8,128)S(1)} %get-tuple-element.9, ...), kind=kLoop, calls=%fused_computation.85 | loop fusion | flops 81782272 | bytes 71462912 | tf_op jit(solution)/shard_map/reduce_sum | solution.py:128
  681.7 28.3 %fusion.55 = bf16[1,4,1024,512]{3,2,1,0:T(8,128)(2,1)} fusion(f32[4,1024]{1,0:T(4,128)S(1)} %copy-done.36, f32[512]{0:T(512)S(1)} %bitcast.314, f32[512]{0:T(512)S(1)} %bitcast.317, f32[512]{0:T(512)S(1)} %bitcast.320, f32[4,1024,512]{2,1,0:T(8,128)} %get-tuple-element.94, f32[512]{0:T(512)S(1)} %bitcast.323, f32[512]{0:T(512)S(1)} %bitcast.326, ...), kind=kLoop, calls=%fused_computation.189 | loop fusion | flops 35651584 | bytes 16807936 | tf_op jit(solution)/shard_map/stack | solution.py:173
  710.1 68.5 %fusion.52 = (bf16[1,4,1024,512]{3,2,1,0:T(8,128)(2,1)}, bf16[1,4,1024,512]{3,2,1,0:T(8,128)(2,1)}, bf16[1,4,1024,512]{3,2,1,0:T(8,128)(2,1)}) fusion(f32[4,1024]{1,0:T(4,128)S(1)} %copy-done.30, f32[512]{0:T(512)S(1)} %bitcast.315, f32[512]{0:T(512)S(1)} %bitcast.318, f32[512]{0:T(512)S(1)} %bitcast.321, f32[4,1024,512]{2,1,0:T(8,128)} %get-tuple-element.175, ...), kind=kLoop, calls=%fused_computation.186 | loop fusion | flops 106954752 | bytes 50395136 | tf_op jit(solution)/shard_map/stack | solution.py:173
  778.6 14.0 %pad_maximum_fusion.1 = bf16[4,4,1024,512]{3,2,1,0:T(8,128)(2,1)} fusion(bf16[1,4,1024,512]{3,2,1,0:T(8,128)(2,1)} %fusion.55, bf16[1,4,1024,512]{3,2,1,0:T(8,128)(2,1)} %get-tuple-element.128, bf16[1,4,1024,512]{3,2,1,0:T(8,128)(2,1)} %get-tuple-element.127, bf16[1,4,1024,512]{3,2,1,0:T(8,128)(2,1)} %get-tuple-element.126), kind=kLoop, calls=%fused_computation.1 | loop fusion | flops 25165824 | bytes 33554432 | tf_op jit(solution)/shard_map/stack | solution.py:173
  792.6 14.5 %reduce_sum.671 = bf16[4096,512]{1,0:T(8,128)(2,1)} reduce(bf16[8,4096,512]{2,1,0:T(8,128)(2,1)} %bitcast.291, bf16[]{:T(256)} %constant.115.clone.1), dimensions={0}, to_apply=%region_11.12 | reduce | flops 14680064 | bytes 37748736 | tf_op jit(solution)/shard_map/reduce_sum | solution.py:100
  807.0 18.0 %all-gather.13.cloned.1.call-done = bf16[32768,512]{1,0:T(8,128)(2,1)} async-done(((bf16[4096,512]{1,0:T(8,128)(2,1)}), bf16[32768,512]{1,0:T(8,128)(2,1)}) %all-gather.13.cloned.1.call-update) | async-done | bytes 33554448 | tf_op jit(solution)/shard_map/all_gather | solution.py:100
  825.0 16.5 %reduce_sum.668 = bf16[4096,512]{1,0:T(8,128)(2,1)} reduce(bf16[8,4096,512]{2,1,0:T(8,128)(2,1)} %bitcast.292, bf16[]{:T(256)} %constant.115.clone.1), dimensions={0}, to_apply=%region_8.9 | reduce | flops 14680064 | bytes 37748736 | tf_op jit(solution)/shard_map/reduce_sum | solution.py:100
  841.5 146.2 %all-gather.9.cloned.1.call-done = bf16[32768,512]{1,0:T(8,128)(2,1)} async-done(((bf16[4096,512]{1,0:T(8,128)(2,1)}), bf16[32768,512]{1,0:T(8,128)(2,1)}) %all-gather.9.cloned.1.call-update) | async-done | bytes 33554448 | tf_op jit(solution)/shard_map/all_gather | solution.py:100
  987.7 16.8 %reduce_sum.662 = bf16[4096,512]{1,0:T(8,128)(2,1)} reduce(bf16[8,4096,512]{2,1,0:T(8,128)(2,1)} %bitcast.293, bf16[]{:T(256)} %constant.115.clone.1), dimensions={0}, to_apply=%region_2.3 | reduce | flops 14680064 | bytes 37748736 | tf_op jit(solution)/shard_map/reduce_sum | solution.py:100
  1004.6 145.9 %all-gather.11.cloned.1.call-done = bf16[32768,512]{1,0:T(8,128)(2,1)} async-done(((bf16[4096,512]{1,0:T(8,128)(2,1)}), bf16[32768,512]{1,0:T(8,128)(2,1)}) %all-gather.11.cloned.1.call-update) | async-done | bytes 33554448 | tf_op jit(solution)/shard_map/all_gather | solution.py:100
  1150.5 14.2 %reduce_sum.665 = bf16[4096,512]{1,0:T(8,128)(2,1)} reduce(bf16[8,4096,512]{2,1,0:T(8,128)(2,1)} %bitcast.294, bf16[]{:T(256)} %constant.115.clone.1), dimensions={0}, to_apply=%region_5.6 | reduce | flops 14680064 | bytes 37748736 | tf_op jit(solution)/shard_map/reduce_sum | solution.py:100
  1164.6 12.1 fusion.14
  1177.8 13.5 %fusion.1 = (bf16[1,4,1024,512]{3,2,1,0:T(8,128)(2,1)S(1)}, bf16[1,4,1024,512]{3,2,1,0:T(8,128)(2,1)S(1)}, bf16[1,4,1024,512]{3,2,1,0:T(8,128)(2,1)S(1)}, bf16[1,4,1024,512]{3,2,1,0:T(8,128)(2,1)S(1)}) fusion(bf16[1,4,1024,512]{3,2,1,0:T(8,128)(2,1)} %bitcast.289, f32[4,1024]{1,0:T(4,128)S(1)} %copy-done.30, f32[512]{0:T(512)S(1)} %bitcast.335, ...), kind=kLoop, calls=%fused_computation.11 | loop fusion | flops 58720256 | bytes 50401280 | tf_op jit(solution)/shard_map/convert_element_type | solution.py:113
  1191.3 7.0 pad_maximum_fusion
  (285 shorter events, 98.7 us)
Async XLA Ops:
  8.0 300.7 %reduce-scatter.12.cloned.1.call-start = ((), (), s32[]{:S(2)}) async-start(), calls=%async_computation.8 | async-start | bytes 327680
  24.5 46.6 %copy-start.65 = (f32[1,512]{1,0:T(1,128)}, f32[1,512]{1,0:T(1,128)S(1)}, u32[]{:S(2)}) copy-start(f32[1,512]{1,0:T(1,128)S(1)} %get-tuple-element.144) | copy-start | bytes 6148
  24.5 46.6 %copy-start.67 = (f32[1,512]{1,0:T(1,128)}, f32[1,512]{1,0:T(1,128)S(1)}, u32[]{:S(2)}) copy-start(f32[1,512]{1,0:T(1,128)S(1)} %get-tuple-element.145) | copy-start | bytes 6148
  24.5 46.6 %copy-start.69 = (f32[1,512]{1,0:T(1,128)}, f32[1,512]{1,0:T(1,128)S(1)}, u32[]{:S(2)}) copy-start(f32[1,512]{1,0:T(1,128)S(1)} %get-tuple-element.146) | copy-start | bytes 6148
  24.5 46.6 %copy-start.71 = (f32[1,512]{1,0:T(1,128)}, f32[1,512]{1,0:T(1,128)S(1)}, u32[]{:S(2)}) copy-start(f32[1,512]{1,0:T(1,128)S(1)} %get-tuple-element.147) | copy-start | bytes 6148
  24.5 46.6 %copy-start.73 = (f32[1,512]{1,0:T(1,128)}, f32[1,512]{1,0:T(1,128)S(1)}, u32[]{:S(2)}) copy-start(f32[1,512]{1,0:T(1,128)S(1)} %get-tuple-element.148) | copy-start | bytes 6148
  24.5 46.6 %copy-start.75 = (f32[1,512]{1,0:T(1,128)}, f32[1,512]{1,0:T(1,128)S(1)}, u32[]{:S(2)}) copy-start(f32[1,512]{1,0:T(1,128)S(1)} %get-tuple-element.149) | copy-start | bytes 6148
  24.5 46.6 %copy-start.77 = (f32[1,512]{1,0:T(1,128)}, f32[1,512]{1,0:T(1,128)S(1)}, u32[]{:S(2)}) copy-start(f32[1,512]{1,0:T(1,128)S(1)} %get-tuple-element.150) | copy-start | bytes 6148
  24.5 143.5 %copy-start.55 = (f32[1,512]{1,0:T(1,128)}, f32[1,512]{1,0:T(1,128)S(1)}, u32[]{:S(2)}) copy-start(f32[1,512]{1,0:T(1,128)S(1)} %get-tuple-element.143) | copy-start | bytes 6148
  26.4 44.6 %copy-start.29 = (f32[4,1024]{1,0:T(4,128)}, f32[4,1024]{1,0:T(4,128)S(1)}, u32[]{:S(2)}) copy-start(f32[4,1024]{1,0:T(4,128)S(1)} %get-tuple-element.184) | copy-start | bytes 49156
  26.4 44.6 %copy-start.31 = (f32[4,1024]{1,0:T(4,128)}, f32[4,1024]{1,0:T(4,128)S(1)}, u32[]{:S(2)}) copy-start(f32[4,1024]{1,0:T(4,128)S(1)} %get-tuple-element.193) | copy-start | bytes 49156
  27.1 43.9 %copy-start.33 = (f32[4,1024]{1,0:T(4,128)}, f32[4,1024]{1,0:T(4,128)S(1)}, u32[]{:S(2)}) copy-start(f32[4,1024]{1,0:T(4,128)S(1)} %get-tuple-element.188) | copy-start | bytes 49156
  27.2 43.9 %copy-start.35 = (f32[4,1024]{1,0:T(4,128)}, f32[4,1024]{1,0:T(4,128)S(1)}, u32[]{:S(2)}) copy-start(f32[4,1024]{1,0:T(4,128)S(1)} %get-tuple-element.195) | copy-start | bytes 49156
  213.2 40.3 %copy-start.12 = (bf16[4096,192]{0,1:T(8,128)(2,1)}, bf16[4096,192]{0,1:T(8,128)(2,1)S(1)}, u32[]{:S(2)}) copy-start(bf16[4096,192]{0,1:T(8,128)(2,1)S(1)} %multiply_convert_fusion) | copy-start | bytes 4718596
  255.5 54.2 %reduce-scatter.10.cloned.1.call-start = ((), (), s32[]{:S(2)}) async-start(), calls=%async_computation.7 | async-start | bytes 327680
  267.3 232.6 %all-reduce.11.cloned.1.call-start = ((), (), s32[]{:S(2)}) async-start(), calls=%async_computation.10 | async-start | bytes 33554432 | tf_op jit(solution)/shard_map/psum | solution.py:111
  282.1 510.5 %all-gather.15.cloned.1.call-start = ((), (), s32[]{:S(2)}) async-start(), calls=%async_computation.6 | async-start | bytes 37748736 | tf_op jit(solution)/shard_map/all_gather | solution.py:100
  287.3 537.7 %all-gather.13.cloned.1.call-start = ((), (), s32[]{:S(2)}) async-start(), calls=%async_computation.5 | async-start | bytes 37748736 | tf_op jit(solution)/shard_map/all_gather | solution.py:100
  292.2 695.5 %all-gather.9.cloned.1.call-start = ((), (), s32[]{:S(2)}) async-start(), calls=%async_computation.3 | async-start | bytes 37748736 | tf_op jit(solution)/shard_map/all_gather | solution.py:100
  295.5 854.9 %all-gather.11.cloned.1.call-start = ((), (), s32[]{:S(2)}) async-start(), calls=%async_computation.4 | async-start | bytes 37748736 | tf_op jit(solution)/shard_map/all_gather | solution.py:100
  298.9 201.0 %copy-start.56 = (f32[1,512]{1,0:T(1,128)S(1)}, f32[1,512]{1,0:T(1,128)}, u32[]{:S(2)}) copy-start(f32[1,512]{1,0:T(1,128)} %copy-done.55) | copy-start | bytes 6148
  299.0 899.4 %reduce-scatter.14.cloned.1.call-start = ((), (), s32[]{:S(2)}) async-start(), calls=%async_computation.9 | async-start | bytes 163840
  525.0 34.9 %copy-start.44 = (f32[4,1024]{1,0:T(4,128)S(1)}, f32[4,1024]{1,0:T(4,128)}, u32[]{:S(2)}) copy-start(f32[4,1024]{1,0:T(4,128)} %copy-done.43) | copy-start | bytes 49156
  525.0 34.9 %copy-start.54 = (f32[4,1024]{1,0:T(4,128)S(1)}, f32[4,1024]{1,0:T(4,128)}, u32[]{:S(2)}) copy-start(f32[4,1024]{1,0:T(4,128)} %copy-done.53) | copy-start | bytes 49156
  634.7 46.9 %copy-start.3 = (f32[4,1024,512]{2,1,0:T(8,128)}, f32[4,1024,512]{2,1,0:T(8,128)S(1)}, u32[]{:S(2)}) copy-start(f32[4,1024,512]{2,1,0:T(8,128)S(1)} %get-tuple-element.91) | copy-start | bytes 25165828
  634.8 46.9 %copy-start.66 = (f32[1,512]{1,0:T(1,128)S(1)}, f32[1,512]{1,0:T(1,128)}, u32[]{:S(2)}) copy-start(f32[1,512]{1,0:T(1,128)} %copy-done.65) | copy-start | bytes 6148
  634.8 46.9 %copy-start.68 = (f32[1,512]{1,0:T(1,128)S(1)}, f32[1,512]{1,0:T(1,128)}, u32[]{:S(2)}) copy-start(f32[1,512]{1,0:T(1,128)} %copy-done.67) | copy-start | bytes 6148
  634.8 46.9 %copy-start.70 = (f32[1,512]{1,0:T(1,128)S(1)}, f32[1,512]{1,0:T(1,128)}, u32[]{:S(2)}) copy-start(f32[1,512]{1,0:T(1,128)} %copy-done.69) | copy-start | bytes 6148
  634.8 46.9 %copy-start.72 = (f32[1,512]{1,0:T(1,128)S(1)}, f32[1,512]{1,0:T(1,128)}, u32[]{:S(2)}) copy-start(f32[1,512]{1,0:T(1,128)} %copy-done.71) | copy-start | bytes 6148
  634.9 46.9 %copy-start.74 = (f32[1,512]{1,0:T(1,128)S(1)}, f32[1,512]{1,0:T(1,128)}, u32[]{:S(2)}) copy-start(f32[1,512]{1,0:T(1,128)} %copy-done.73) | copy-start | bytes 6148
  634.9 46.9 %copy-start.76 = (f32[1,512]{1,0:T(1,128)S(1)}, f32[1,512]{1,0:T(1,128)}, u32[]{:S(2)}) copy-start(f32[1,512]{1,0:T(1,128)} %copy-done.75) | copy-start | bytes 6148
  634.9 46.9 %copy-start.78 = (f32[1,512]{1,0:T(1,128)S(1)}, f32[1,512]{1,0:T(1,128)}, u32[]{:S(2)}) copy-start(f32[1,512]{1,0:T(1,128)} %copy-done.77) | copy-start | bytes 6148
  (70 other events, 765.3 us)
Sparse Core Ops, SparseCore 0:
  255.6 18.2 reduce-scatter.11
  276.1 17.8 reduce-scatter.9
  1177.9 19.1 reduce-scatter.13
Sparse Core Ops, SparseCore 1:
  282.2 217.6 all-reduce.10
  501.8 160.6 all-gather.14
  664.4 160.6 all-gather.12
  827.1 160.6 all-gather.8
  989.8 160.6 all-gather.10
